TPU v7x, 32 devices: a whole 2x2x4 slice. The times are simulated.
32 devices in a mesh: layer: 2 (over x), feat: 4 (over z), tok: 4 (over y, core).
Axes of the slice: x: 2, y: 2, z: 4, core: 2. Of those that a mesh axis runs over, the one named last changes fastest.
Arguments:
- resid: bfloat16 [2, 1024, 2304], P('layer', 'tok', 'feat'), may hold values from -6 to 6
- norm_gain: bfloat16 [2, 2304], P('layer', 'feat'), may hold values from 0.5 to 2
- prev_codes: bfloat16 [1024, 16384], P('tok', 'feat'), may hold values from 0 to 1.5
- feature_mask: int32 [2, 8, 128], P('layer', 'tok', 'feat'), may hold values 0 or 1
- w_gate: bfloat16 [2, 2304, 9216], P('layer', 'tok', 'feat'), may hold values from -0.125 to 0.125
- w_up: bfloat16 [2, 2304, 9216], P('layer', 'tok', 'feat'), may hold values from -0.125 to 0.125
- w_down: bfloat16 [2, 9216, 2304], P('layer', 'feat', 'tok'), may hold values from -0.0625 to 0.0625
- enc_weight: bfloat16 [2, 2304, 16384], P('layer', 'tok', 'feat'), may hold values from -0.125 to 0.125
- enc_bias: float32 [2, 16384], P('layer', 'feat'), may hold values from -3 to 3
- dec_own: bfloat16 [2, 16384, 2304], P('layer', 'feat', 'tok'), may hold values from -0.046875 to 0.046875
- dec_prev: bfloat16 [2, 16384, 2304], P('layer', 'feat', 'tok'), may hold values from -0.046875 to 0.046875
Outputs:
- grad_enc: float32 [2, 2304, 16384], P('layer', 'tok', 'feat')
- grad_bias: float32 [2, 16384], P('layer', 'feat')
- grad_own: float32 [2, 16384, 2304], P('layer', 'feat', 'tok')
- grad_prev: float32 [2, 16384, 2304], P('layer', 'feat', 'tok')
All inputs are finite; a program needn't handle non-finite values. No bound on the sum of `feature_mask` on one device may be relied on, other than what follows from the above.
Results may differ from a plain program's by a relative error of at most 0.0063.
Values may be sent and summed in bfloat16 or wider, within the bound.
A program may use at most 256 MiB of HBM per device.

v0:
```python
import math
import jax
import jax.numpy as jnp
from jax import lax
from jax.sharding import PartitionSpec as P

TILE = 128
TBLK = 128


def passed_along(value, axis, steps):
    count = lax.axis_size(axis)
    leading, last = (max(0, -steps), min(count, count - steps))
    return lax.ppermute(value, axis, [(source, source + steps) for source in range(leading, last)])


def block_keep(block_mask, height, breadth):
    blocks = block_mask.astype(jnp.float32)
    spread = jnp.broadcast_to(
        blocks[:, None, :, None], (blocks.shape[0], TBLK, blocks.shape[1], TILE)
    )
    return spread.reshape(height, breadth)


def local(
    resid,
    norm_gain,
    prev_codes,
    feature_mask,
    w_gate,
    w_up,
    w_down,
    enc_weight,
    enc_bias,
    dec_own,
    dec_prev,
):
    gathered, gains = (
        lax.all_gather(resid[0], "feat", axis=1, tiled=True),
        lax.all_gather(norm_gain, "feat", axis=1, tiled=True),
    )
    stream = gathered.astype(jnp.float32)
    normed = (
        stream
        * lax.rsqrt(jnp.mean(stream * stream, axis=1, keepdims=True) + 1e-06)
        * gains[0].astype(jnp.float32)
    ).astype(jnp.bfloat16)
    height = normed.shape[0]
    feat_local = enc_weight.shape[2]
    segments = (
        lax.all_gather(w_gate[0], "tok", axis=0, tiled=True),
        lax.all_gather(w_up[0], "tok", axis=0, tiled=True),
        lax.all_gather(enc_weight[0], "tok", axis=0, tiled=True),
    )
    gate_sum, up_sum, enc_sum = tuple(
        (jnp.dot(normed, segment, preferred_element_type=jnp.float32) for segment in segments)
    )
    hidden = (jax.nn.gelu(gate_sum, approximate=True) * up_sum).astype(jnp.bfloat16)
    preact = enc_sum + enc_bias[0]
    active = jnp.maximum(preact, 0.0)
    keeper = block_keep(feature_mask[0], height, feat_local)
    codes = (active * active * keeper).astype(jnp.bfloat16)
    shifted = passed_along(codes, "layer", 1)
    source = jnp.where(lax.axis_index("layer") == 0, prev_codes, shifted)
    own_full, prev_full = (
        lax.all_gather(dec_own[0], "tok", axis=1, tiled=True),
        lax.all_gather(dec_prev[0], "tok", axis=1, tiled=True),
    )
    partial_value = (
        jnp.dot(codes, own_full, preferred_element_type=jnp.float32)
        + jnp.dot(source, prev_full, preferred_element_type=jnp.float32)
        - jnp.dot(
            hidden,
            lax.all_gather(w_down[0], "tok", axis=1, tiled=True),
            preferred_element_type=jnp.float32,
        )
    )
    error = lax.psum(partial_value, "feat").astype(jnp.bfloat16)
    own_back = jnp.dot(error, own_full.T, preferred_element_type=jnp.float32)
    prev_back = jnp.dot(error, prev_full.T, preferred_element_type=jnp.float32)
    later = passed_along(prev_back.astype(jnp.bfloat16), "layer", -1).astype(prev_back.dtype)
    back = own_back + later
    factor = 1.0 / math.sqrt(height * lax.axis_size("tok"))
    pregrad = (back * keeper * (2.0 * active) * factor).astype(jnp.bfloat16)
    normed_cols = lax.all_to_all(normed, "tok", split_axis=1, concat_axis=0, tiled=True)
    error_cols = lax.all_to_all(error, "tok", split_axis=1, concat_axis=0, tiled=True)
    codes_all, source_all = (
        lax.all_gather(codes, "tok", axis=0, tiled=True),
        lax.all_gather(source, "tok", axis=0, tiled=True),
    )
    pregrad_all = lax.all_gather(pregrad, "tok", axis=0, tiled=True)
    grad_enc = jnp.dot(normed_cols.T, pregrad_all, preferred_element_type=jnp.float32)
    grad_bias = jnp.sum(pregrad_all.astype(jnp.float32), axis=0)
    grad_own = jnp.dot(codes_all.T, error_cols, preferred_element_type=jnp.float32) * factor
    grad_prev = jnp.dot(source_all.T, error_cols, preferred_element_type=jnp.float32) * factor
    return (grad_enc[None], grad_bias[None], grad_own[None], grad_prev[None])


def solution(mesh):
    in_specs = (
        P("layer", "tok", "feat"),
        P("layer", "feat"),
        P("tok", "feat"),
        P("layer", "tok", "feat"),
        P("layer", "tok", "feat"),
        P("layer", "tok", "feat"),
        P("layer", "feat", "tok"),
        P("layer", "tok", "feat"),
        P("layer", "feat"),
        P("layer", "feat", "tok"),
        P("layer", "feat", "tok"),
    )
    out_specs = (
        P("layer", "tok", "feat"),
        P("layer", "feat"),
        P("layer", "feat", "tok"),
        P("layer", "feat", "tok"),
    )
    return jax.shard_map(local, mesh=mesh, in_specs=in_specs, out_specs=out_specs, check_vma=False)
```

profile of v0, /device:TPU:0, one launch (start us, length us, event | category | flops | bytes accessed | tf_op | source)
XLA Modules:
  0.0 905.5 jit_solution(4202386493531622728)
XLA Ops:
  7.2 0.7 all-gather.24.cloned.1.call-update
  7.9 0.0 all-gather.26.cloned.1.call-start
  7.9 0.7 all-gather.26.cloned.1.call-update
  8.7 0.7 all-gather.32.cloned.1.call-update
  9.4 0.5 all-gather.28.cloned.1.call-update
  10.0 0.5 all-gather.30.cloned.1.call-update
  10.6 0.5 all-gather.34.cloned.1.call-update
  11.2 0.7 all-gather.36.cloned.1.call-update
  11.9 0.0 all-gather.20.cloned.1.call-start
  12.0 0.6 dynamic-slice
  13.3 0.2 dynamic-update-slice
  13.5 14.1 %all-reduce = bf16[2304]{0:T(1024)(128)(2,1)S(1)} all-reduce(bf16[2304]{0:T(1024)(128)(2,1)S(1)} %dynamic-update-slice), channel_id=1, replica_groups=mesh['layer'=2,'feat'=4,'tok'=4] {'feat'}, use_global_device_ids=true, to_apply=%add | all-reduce | flops 2304 | bytes 9216
  27.6 15.1 %all-gather.24.cloned.1.call-done = bf16[1,256,2304]{1,2,0:T(8,128)(2,1)} async-done(((bf16[1,256,576]{1,2,0:T(8,128)(2,1)}), bf16[1,256,2304]{1,2,0:T(8,128)(2,1)}) %all-gather.24.cloned.1.call-update) | async-done | bytes 1179664 | tf_op jit(solution)/shard_map/all_gather | solution.py:39
  42.7 1.6 fusion.41
  44.4 2.7 fusion.43
  47.0 116.6 %all-gather.26.cloned.1.call-done = bf16[1,2304,4096]{2,1,0:T(8,128)(2,1)} async-done(((bf16[1,576,4096]{2,1,0:T(8,128)(2,1)}), bf16[1,2304,4096]{2,1,0:T(8,128)(2,1)}) %all-gather.26.cloned.1.call-update) | async-done | bytes 18874384 | tf_op jit(solution)/shard_map/all_gather | solution.py:53
  163.6 0.6 broadcast_in_dim.20
  164.2 16.5 %fusion.25 = (bf16[256,4096]{1,0:T(8,128)(2,1)}, f32[256,4096]{1,0:T(8,128)}) fusion(f32[32,8,32,128]{3,2,1,0:T(8,128)S(1)} %bitcast.93, f32[4096]{0:T(1024)S(1)} %bitcast.100, bf16[256,2304]{0,1:T(8,128)(2,1)} %fusion.43, bf16[1,2304,4096]{2,1,0:T(8,128)(2,1)} %all-gather.26.cloned.1.call-done), kind=kOutput, calls=%fused_computation.25 | convolution fusion | flops 4837081088 | bytes 30556160 | tf_op jit(solution)/shard_map/dot_general | solution.py:56
  180.7 0.0 all-gather.22.cloned.1.call-start
  180.8 4.7 collective-permute-start
  185.5 50.6 %all-gather.32.cloned.1.call-done = bf16[1,2304,2304]{2,1,0:T(8,128)(2,1)} async-done(((bf16[1,576,2304]{2,1,0:T(8,128)(2,1)}), bf16[1,2304,2304]{2,1,0:T(8,128)(2,1)}) %all-gather.32.cloned.1.call-update) | async-done | bytes 10616848 | tf_op jit(solution)/shard_map/all_gather | solution.py:51
  236.1 9.3 %fusion.50 = f32[256,2304]{1,0:T(8,128)} fusion(bf16[256,2304]{0,1:T(8,128)(2,1)} %fusion.43, bf16[1,2304,2304]{2,1,0:T(8,128)(2,1)} %all-gather.32.cloned.1.call-done), kind=kOutput, calls=%fused_computation.45 | convolution fusion | flops 2722627584 | bytes 14155776 | tf_op jit(solution)/shard_map/dot_general | solution.py:56
  245.4 1.5 broadcast_select_fusion
  247.0 0.2 all-gather.18.cloned.1.call-start
  247.2 110.3 %all-gather.28.cloned.1.call-done = bf16[1,4096,2304]{1,2,0:T(8,128)(2,1)} async-done(((bf16[1,4096,576]{1,2,0:T(8,128)(2,1)}), bf16[1,4096,2304]{1,2,0:T(8,128)(2,1)}) %all-gather.28.cloned.1.call-update) | async-done | bytes 18874384 | tf_op jit(solution)/shard_map/all_gather | solution.py:66
  357.5 10.4 %fusion.6 = f32[256,2304]{1,0:T(8,128)} fusion(bf16[256,4096]{1,0:T(8,128)(2,1)S(1)} %copy-done.2, bf16[1,4096,2304]{1,2,0:T(8,128)(2,1)} %all-gather.28.cloned.1.call-done), kind=kOutput, calls=%fused_computation.6 | convolution fusion | flops 4831838208 | bytes 23330816 | tf_op jit(solution)/shard_map/dot_general | solution.py:70
  368.0 111.0 %all-gather.30.cloned.1.call-done = bf16[1,4096,2304]{1,2,0:T(8,128)(2,1)} async-done(((bf16[1,4096,576]{1,2,0:T(8,128)(2,1)}), bf16[1,4096,2304]{1,2,0:T(8,128)(2,1)}) %all-gather.30.cloned.1.call-update) | async-done | bytes 18874384 | tf_op jit(solution)/shard_map/all_gather | solution.py:67
  479.0 11.7 %fusion.35 = f32[256,2304]{1,0:T(8,128)} fusion(f32[256,2304]{1,0:T(8,128)} %fusion.6, bf16[256,4096]{1,0:T(8,128)(2,1)} %broadcast_select_fusion, bf16[1,4096,2304]{1,2,0:T(8,128)(2,1)} %all-gather.30.cloned.1.call-done), kind=kOutput, calls=%fused_computation.31 | convolution fusion | flops 4832428032 | bytes 25690112 | tf_op jit(solution)/shard_map/dot_general | solution.py:71
  490.7 60.7 %all-gather.34.cloned.1.call-done = bf16[1,2304,2304]{2,1,0:T(8,128)(2,1)} async-done(((bf16[1,576,2304]{2,1,0:T(8,128)(2,1)}), bf16[1,2304,2304]{2,1,0:T(8,128)(2,1)}) %all-gather.34.cloned.1.call-update) | async-done | bytes 10616848 | tf_op jit(solution)/shard_map/all_gather | solution.py:52
  551.3 72.5 %all-gather.36.cloned.1.call-done = bf16[1,2304,2304]{1,2,0:T(8,128)(2,1)} async-done(((bf16[1,2304,576]{1,2,0:T(8,128)(2,1)}), bf16[1,2304,2304]{1,2,0:T(8,128)(2,1)}) %all-gather.36.cloned.1.call-update) | async-done | bytes 10616848 | tf_op jit(solution)/shard_map/all_gather | solution.py:74
  623.9 15.3 %fusion.32 = f32[256,2304]{1,0:T(8,128)S(1)} fusion(f32[256,2304]{1,0:T(8,128)} %fusion.35, bf16[1,2304,2304]{1,2,0:T(8,128)(2,1)} %all-gather.36.cloned.1.call-done, f32[256,2304]{1,0:T(8,128)} %fusion.50, bf16[256,2304]{0,1:T(8,128)(2,1)} %fusion.43, bf16[1,2304,2304]{2,1,0:T(8,128)(2,1)} %all-gather.34.cloned.1.call-done), kind=kOutput, calls=%fused_computation.30 | convolution fusion | flops 5437587456 | bytes 29491200 | tf_op jit(solution)/shard_map/dot_general | solution.py:72
  639.2 87.3 %all-reduce.2 = bf16[256,2304]{1,0:T(8,128)(2,1)S(1)} all-reduce(f32[256,2304]{1,0:T(8,128)S(1)} %fusion.32), channel_id=1, replica_groups=mesh['layer'=2,'feat'=4,'tok'=4] {'feat'}, use_global_device_ids=true, to_apply=%region_1.2 | all-reduce | flops 589824 | bytes 3538944 | tf_op jit(solution)/shard_map/psum | solution.py:78
  726.5 10.1 %fusion.22 = bf16[256,4096]{1,0:T(8,128)(2,1)S(1)} fusion(bf16[256,2304]{1,0:T(8,128)(2,1)S(1)} %all-reduce.2, bf16[1,4096,2304]{1,2,0:T(8,128)(2,1)} %all-gather.30.cloned.1.call-done), kind=kOutput, calls=%fused_computation.22 | convolution fusion | flops 4832886784 | bytes 22151168 | tf_op jit(solution)/shard_map/dot_general | solution.py:80
  736.6 1.3 collective-permute-start.1
  737.9 46.5 %collective-permute-done.1 = bf16[256,4096]{1,0:T(8,128)(2,1)S(1)} collective-permute-done((bf16[256,4096]{1,0:T(8,128)(2,1)S(1)}, bf16[256,4096]{1,0:T(8,128)(2,1)S(1)}, u32[]{:S(2)}, u32[]{:S(2)}) %collective-permute-start.1) | collective-permute-done | bytes 2097184 | tf_op jit(solution)/shard_map/ppermute | solution.py:14
  784.4 16.2 %fusion.28 = bf16[256,4096]{1,0:T(8,128)(2,1)} fusion(f32[256,4096]{1,0:T(8,128)S(1)} %copy-done.4, bf16[256,4096]{1,0:T(8,128)(2,1)S(1)} %collective-permute-done.1, f32[32,8,32,128]{3,2,1,0:T(8,128)S(1)} %bitcast.94, bf16[256,2304]{1,0:T(8,128)(2,1)S(1)} %all-reduce.2, bf16[1,4096,2304]{1,2,0:T(8,128)(2,1)} %all-gather.28.cloned.1.call-done), kind=kOutput, calls=%fused_computation.28 | convolution fusion | flops 4839178240 | bytes 32636928 | tf_op jit(solution)/shard_map/dot_general | solution.py:79
  800.7 3.5 all-to-all-start
  804.2 1.4 copy.19
  805.7 25.4 %all-to-all-done = bf16[256,4,576]{0,2,1:T(8,128)(2,1)S(1)} async-done(((bf16[256,4,576]{0,2,1:T(8,128)(2,1)}), bf16[256,4,576]{0,2,1:T(8,128)(2,1)S(1)}, u32[]{:S(2)}, u32[]{:S(2)}) %all-to-all-start) | async-done | bytes 1179680 | tf_op jit(solution)/shard_map/all_to_all | solution.py:85
  831.1 3.8 all-to-all-start.1
  834.9 0.1 copy.21
  835.0 28.4 %all-to-all-done.1 = bf16[256,4,576]{0,2,1:T(8,128)(2,1)S(1)} async-done(((bf16[256,4,576]{0,2,1:T(8,128)(2,1)}), bf16[256,4,576]{0,2,1:T(8,128)(2,1)S(1)}, u32[]{:S(2)}, u32[]{:S(2)}) %all-to-all-start.1) | async-done | bytes 1179680 | tf_op jit(solution)/shard_map/all_to_all | solution.py:86
  863.5 0.1 copy.22
  863.7 10.9 %multiply_bitcast_fusion.1 = f32[1,4096,576]{1,2,0:T(8,128)} fusion(bf16[1024,576]{0,1:T(8,128)(2,1)S(1)} %bitcast.98, bf16[1024,4096]{1,0:T(8,128)(2,1)} %all-gather.20.cloned.1.call-done), kind=kOutput, calls=%fused_computation.18 | convolution fusion | flops 4834197504 | bytes 19005440 | tf_op jit(solution)/shard_map/dot_general | solution.py:94
  874.5 10.8 %multiply_bitcast_fusion = f32[1,4096,576]{1,2,0:T(8,128)} fusion(bf16[1024,576]{0,1:T(8,128)(2,1)S(1)} %bitcast.99, bf16[1024,4096]{1,0:T(8,128)(2,1)} %all-gather.22.cloned.1.call-done), kind=kOutput, calls=%fused_computation.17 | convolution fusion | flops 4834197504 | bytes 19005440 | tf_op jit(solution)/shard_map/dot_general | solution.py:95
  885.4 5.3 convert_reduce_fusion
  890.7 0.4 copy-done.3
  891.1 7.5 convolution_bitcast_fusion
  (37 shorter events, 0.4 us)
Async XLA Ops:
  7.2 35.6 %all-gather.24.cloned.1.call-start = ((), (), s32[]{:S(2)}) async-start(), calls=%async_computation.5 | async-start | bytes 1474560 | tf_op jit(solution)/shard_map/all_gather | solution.py:39
  7.9 155.7 %all-gather.26.cloned.1.call-start = ((), (), s32[]{:S(2)}) async-start(), calls=%async_computation.6 | async-start | bytes 23592960 | tf_op jit(solution)/shard_map/all_gather | solution.py:53
  8.6 227.4 %all-gather.32.cloned.1.call-start = ((), (), s32[]{:S(2)}) async-start(), calls=%async_computation.9 | async-start | bytes 13271040 | tf_op jit(solution)/shard_map/all_gather | solution.py:51
  9.4 348.2 %all-gather.28.cloned.1.call-start = ((), (), s32[]{:S(2)}) async-start(), calls=%async_computation.7 | async-start | bytes 23592960 | tf_op jit(solution)/shard_map/all_gather | solution.py:66
  10.0 469.0 %all-gather.30.cloned.1.call-start = ((), (), s32[]{:S(2)}) async-start(), calls=%async_computation.8 | async-start | bytes 23592960 | tf_op jit(solution)/shard_map/all_gather | solution.py:67
  10.5 1.4 copy-start.9
  10.6 2.7 copy-start.7
  10.6 17.0 %copy-start.8 = (s32[1,2,32]{2,1,0:T(2,128)S(1)}, s32[1,2,32]{2,1,0:T(2,128)}, u32[]{:S(2)}) copy-start(s32[1,2,32]{2,1,0:T(2,128)} %param.14) | copy-start | bytes 772
  10.6 540.8 %all-gather.34.cloned.1.call-start = ((), (), s32[]{:S(2)}) async-start(), calls=%async_computation.10 | async-start | bytes 13271040 | tf_op jit(solution)/shard_map/all_gather | solution.py:52
  11.2 612.7 %all-gather.36.cloned.1.call-start = ((), (), s32[]{:S(2)}) async-start(), calls=%async_computation.11 | async-start | bytes 13271040 | tf_op jit(solution)/shard_map/all_gather | solution.py:74
  11.9 851.7 %all-gather.20.cloned.1.call-start = ((), (), s32[]{:S(2)}) async-start(), calls=%async_computation.3 | async-start | bytes 10485760 | tf_op jit(solution)/shard_map/all_gather | solution.py:88
  47.0 117.2 %copy-start.6 = (f32[1,4096]{1,0:T(1,128)S(1)}, f32[1,4096]{1,0:T(1,128)}, u32[]{:S(2)}) copy-start(f32[1,4096]{1,0:T(1,128)} %param.19) | copy-start | bytes 49156
  164.2 16.5 %copy-start = (f32[2,128,32,128]{3,2,1,0:T(8,128)}, f32[2,128,32,128]{3,2,1,0:T(8,128)S(1)}, u32[]{:S(2)}) copy-start(f32[2,128,32,128]{3,2,1,0:T(8,128)S(1)} %broadcast_in_dim.20) | copy-start | bytes 12582916
  180.7 693.8 %all-gather.22.cloned.1.call-start = ((), (), s32[]{:S(2)}) async-start(), calls=%async_computation.4 | async-start | bytes 10485760 | tf_op jit(solution)/shard_map/all_gather | solution.py:89
  180.8 64.6 %collective-permute-start = (bf16[256,4096]{1,0:T(8,128)(2,1)}, bf16[256,4096]{1,0:T(8,128)(2,1)}, u32[]{:S(2)}, u32[]{:S(2)}) collective-permute-start(bf16[256,4096]{1,0:T(8,128)(2,1)} %get-tuple-element.4), channel_id=1, source_target_pairs={{0,16},{1,17},{2,18},{3,19},{4,20},{5,21},{6,22},{7,23},{8,24},{9,... | collective-permute-start | bytes 6291464 | tf_op jit(solution)/shard_map/ppermute | solution.py:14
  236.1 9.3 %copy-start.5 = (bf16[256,4096]{1,0:T(8,128)(2,1)S(1)}, bf16[256,4096]{1,0:T(8,128)(2,1)}, u32[]{:S(2)}) copy-start(bf16[256,4096]{1,0:T(8,128)(2,1)} %param.13) | copy-start | bytes 6291460
  245.4 112.1 %copy-start.2 = (bf16[256,4096]{1,0:T(8,128)(2,1)S(1)}, bf16[256,4096]{1,0:T(8,128)(2,1)}, u32[]{:S(2)}) copy-start(bf16[256,4096]{1,0:T(8,128)(2,1)} %get-tuple-element.4) | copy-start | bytes 6291460
  247.0 638.4 %all-gather.18.cloned.1.call-start = ((), (), s32[]{:S(2)}) async-start(), calls=%async_computation.2 | async-start | bytes 10485760 | tf_op jit(solution)/shard_map/all_gather | solution.py:91
  726.5 57.9 %copy-start.1 = (f32[2,128,32,128]{3,2,1,0:T(8,128)S(1)}, f32[2,128,32,128]{3,2,1,0:T(8,128)}, u32[]{:S(2)}) copy-start(f32[2,128,32,128]{3,2,1,0:T(8,128)} %copy-done) | copy-start | bytes 12582916
  726.5 57.9 %copy-start.4 = (f32[256,4096]{1,0:T(8,128)S(1)}, f32[256,4096]{1,0:T(8,128)}, u32[]{:S(2)}) copy-start(f32[256,4096]{1,0:T(8,128)} %get-tuple-element.5) | copy-start | bytes 12582916
  736.6 47.8 %collective-permute-start.1 = (bf16[256,4096]{1,0:T(8,128)(2,1)S(1)}, bf16[256,4096]{1,0:T(8,128)(2,1)S(1)}, u32[]{:S(2)}, u32[]{:S(2)}) collective-permute-start(bf16[256,4096]{1,0:T(8,128)(2,1)S(1)} %fusion.22), channel_id=1, source_target_pairs={{16,0},{17,1},{18,2},{19,3},{20,4},{21,5},{22,6},{23,7},{24,8},{25... | collective-permute-start | bytes 6291464 | tf_op jit(solution)/shard_map/ppermute | solution.py:14
  800.7 30.4 %all-to-all-start = ((bf16[256,4,576]{0,2,1:T(8,128)(2,1)}), bf16[256,4,576]{0,2,1:T(8,128)(2,1)S(1)}, u32[]{:S(2)}, u32[]{:S(2)}) async-start(bf16[256,4,576]{0,2,1:T(8,128)(2,1)} %bitcast.3), calls=%async_computation | async-start | bytes 2359296 | tf_op jit(solution)/shard_map/all_to_all | solution.py:85
  831.1 32.4 %all-to-all-start.1 = ((bf16[256,4,576]{0,2,1:T(8,128)(2,1)}), bf16[256,4,576]{0,2,1:T(8,128)(2,1)S(1)}, u32[]{:S(2)}, u32[]{:S(2)}) async-start(bf16[256,4,576]{0,2,1:T(8,128)(2,1)} %bitcast.15), calls=%async_computation.1 | async-start | bytes 2359296 | tf_op jit(solution)/shard_map/all_to_all | solution.py:86
  885.4 5.8 copy-start.3
Sparse Core Ops, SparseCore 0:
  9.5 33.1 all-gather.23
  44.3 119.2 all-gather.25
  165.1 70.9 all-gather.31
  237.5 119.9 all-gather.27
  359.0 119.9 all-gather.29
  480.4 70.9 all-gather.33
  552.9 70.9 all-gather.35
  625.4 58.2 all-gather.19
  685.3 58.2 all-gather.21
  800.8 78.5 all-gather.17
where the time goes:
time: 906 us; the launch traced here: 905 us
  waiting for transfers between devices  642 us (71%)
  matrix products  119 us (13%)
  blocking collectives  101 us (11%)
  between operations  15 us (2%)
  starting transfers between devices  13.9 us (2%)
  other arithmetic  11.2 us (1%)
    all_gather x1, waiting for transfers between devices, local(): lax.all_gather(enc_weight[0], 'tok', axis=0, tiled=True)  117 us
    all_gather x1, waiting for transfers between devices, local(): lax.all_gather(dec_prev[0], 'tok', axis=1, tiled=True)  111 us
    all_gather x1, waiting for transfers between devices, local(): lax.all_gather(dec_own[0], 'tok', axis=1, tiled=True)  110 us
    psum x1, blocking collectives, local(): error = lax.psum(partial_value, 'feat').astype(jnp.bfloat16)  87.3 us
    all_gather x1, waiting for transfers between devices, local(): lax.all_gather(w_down[0], 'tok', axis=1, tiled=True)  72.5 us
    all_gather x1, waiting for transfers between devices, local(): lax.all_gather(w_up[0], 'tok', axis=0, tiled=True)  60.7 us
    all_gather x1, waiting for transfers between devices, local(): lax.all_gather(w_gate[0], 'tok', axis=0, tiled=True)  50.6 us
    ppermute x2, waiting for transfers between devices, passed_along(): lax.ppermute(value, axis, [(source, source + steps) for source in range(l...  46.5 us
  transfers between devices with their start and end apart: 14, of which 10 were waited for; matrix products, arithmetic and copies ran while one was open for 13% of the time, Pallas kernels for 0%

commit v1 on v0

--- a/solution.py
+++ b/solution.py
@@ -75,7 +75,7 @@
             preferred_element_type=jnp.float32,
         )
     )
-    error = lax.psum(partial_value, "feat").astype(jnp.bfloat16)
+    error = jnp.sum(lax.all_gather(partial_value, "feat"), axis=0).astype(jnp.bfloat16)
     own_back = jnp.dot(error, own_full.T, preferred_element_type=jnp.float32)
     prev_back = jnp.dot(error, prev_full.T, preferred_element_type=jnp.float32)
     later = passed_along(prev_back.astype(jnp.bfloat16), "layer", -1).astype(prev_back.dtype)

time: 906 us -> 1030 us (1.14)
  waiting for transfers between devices: 642 us -> 843 us
  blocking collectives: 101 us -> 14.1 us
    all_gather x0 -> x1, waiting for transfers between devices: none -> 166 us  [local(): lax.all_gather(partial_value, 'feat')]
    psum x1 -> x0, blocking collectives: 87.3 us -> none  [local(): error = lax.psum(partial_value, 'feat').astype(jnp.bfloat16)]
    all_gather x1, waiting for transfers between devices: 0.01 us -> 39 us  [local(): pregrad_all = lax.all_gather(pregrad, 'tok', axis=0, tiled=True)]
  transfers between devices with their start and end apart: 14 -> 15, of which waited for: 10 -> 12; matrix products, arithmetic and copies ran while one was open for 13% -> 11% of each run, Pallas kernels for 0% -> 0%
where the time goes in v1:
time: 1030 us
  waiting for transfers between devices  843 us (82%)
  matrix products  125 us (12%)
  other arithmetic  16.4 us (2%)
  between operations  14.7 us (1%)
  blocking collectives  14.1 us (1%)
  starting transfers between devices  13.8 us (1%)
    all_gather x1, waiting for transfers between devices, local(): lax.all_gather(partial_value, 'feat')  166 us
    all_gather x1, waiting for transfers between devices, local(): lax.all_gather(enc_weight[0], 'tok', axis=0, tiled=True)  117 us
    all_gather x1, waiting for transfers between devices, local(): lax.all_gather(dec_own[0], 'tok', axis=1, tiled=True)  112 us
    all_gather x1, waiting for transfers between devices, local(): lax.all_gather(dec_prev[0], 'tok', axis=1, tiled=True)  109 us
    all_gather x1, waiting for transfers between devices, local(): lax.all_gather(w_down[0], 'tok', axis=1, tiled=True)  72.5 us
    all_gather x1, waiting for transfers between devices, local(): lax.all_gather(w_up[0], 'tok', axis=0, tiled=True)  61 us
    all_gather x1, waiting for transfers between devices, local(): lax.all_gather(w_gate[0], 'tok', axis=0, tiled=True)  51.1 us
    ppermute x2, waiting for transfers between devices, passed_along(): lax.ppermute(value, axis, [(source, source + steps) for source in range(l...  48.2 us
  transfers between devices with their start and end apart: 15, of which 12 were waited for; matrix products, arithmetic and copies ran while one was open for 11% of the time, Pallas kernels for 0%

profile of v1, /device:TPU:0, one launch (start us, length us, event | category | flops | bytes accessed | tf_op | source)
XLA Modules:
  0.0 1030.3 jit_solution(12065468270862980284)
XLA Ops:
  7.2 0.7 all-gather.26.cloned.1.call-update
  7.9 0.7 all-gather.28.cloned.1.call-update
  8.7 0.7 all-gather.34.cloned.1.call-update
  9.4 0.5 all-gather.30.cloned.1.call-update
  10.0 0.5 all-gather.32.cloned.1.call-update
  10.6 0.5 all-gather.36.cloned.1.call-update
  11.2 0.7 all-gather.38.cloned.1.call-update
  12.0 0.6 dynamic-slice
  13.3 0.2 dynamic-update-slice
  13.5 14.1 %all-reduce = bf16[2304]{0:T(1024)(128)(2,1)S(1)} all-reduce(bf16[2304]{0:T(1024)(128)(2,1)S(1)} %dynamic-update-slice), channel_id=1, replica_groups=mesh['layer'=2,'feat'=4,'tok'=4] {'feat'}, use_global_device_ids=true, to_apply=%add | all-reduce | flops 2304 | bytes 9216
  27.6 15.1 %all-gather.26.cloned.1.call-done = bf16[1,256,2304]{1,2,0:T(8,128)(2,1)} async-done(((bf16[1,256,576]{1,2,0:T(8,128)(2,1)}), bf16[1,256,2304]{1,2,0:T(8,128)(2,1)}) %all-gather.26.cloned.1.call-update) | async-done | bytes 1179664 | tf_op jit(solution)/shard_map/all_gather | solution.py:39
  42.7 1.6 fusion.41
  44.4 2.7 fusion.43
  47.0 116.5 %all-gather.28.cloned.1.call-done = bf16[1,2304,4096]{2,1,0:T(8,128)(2,1)} async-done(((bf16[1,576,4096]{2,1,0:T(8,128)(2,1)}), bf16[1,2304,4096]{2,1,0:T(8,128)(2,1)}) %all-gather.28.cloned.1.call-update) | async-done | bytes 18874384 | tf_op jit(solution)/shard_map/all_gather | solution.py:53
  163.6 0.6 broadcast_in_dim.20
  164.2 16.1 %fusion.25 = (bf16[256,4096]{1,0:T(8,128)(2,1)S(1)}, f32[256,4096]{1,0:T(8,128)}) fusion(f32[32,8,32,128]{3,2,1,0:T(8,128)S(1)} %bitcast.94, f32[4096]{0:T(1024)S(1)} %bitcast.102, bf16[256,2304]{0,1:T(8,128)(2,1)} %fusion.43, bf16[1,2304,4096]{2,1,0:T(8,128)(2,1)} %all-gather.28.cloned.1.call-done), kind=kOutput, calls=%fused_computation.25 | convolution fusion | flops 4837081088 | bytes 30556160 | tf_op jit(solution)/shard_map/dot_general | solution.py:56
  180.3 4.7 collective-permute-start
  185.0 51.1 %all-gather.34.cloned.1.call-done = bf16[1,2304,2304]{2,1,0:T(8,128)(2,1)} async-done(((bf16[1,576,2304]{2,1,0:T(8,128)(2,1)}), bf16[1,2304,2304]{2,1,0:T(8,128)(2,1)}) %all-gather.34.cloned.1.call-update) | async-done | bytes 10616848 | tf_op jit(solution)/shard_map/all_gather | solution.py:51
  236.1 9.2 fusion.50
  245.3 112.2 %all-gather.30.cloned.1.call-done = bf16[1,4096,2304]{1,2,0:T(8,128)(2,1)} async-done(((bf16[1,4096,576]{1,2,0:T(8,128)(2,1)}), bf16[1,4096,2304]{1,2,0:T(8,128)(2,1)}) %all-gather.30.cloned.1.call-update) | async-done | bytes 18874384 | tf_op jit(solution)/shard_map/all_gather | solution.py:66
  357.5 10.4 %fusion.6 = f32[256,2304]{1,0:T(8,128)} fusion(bf16[256,4096]{1,0:T(8,128)(2,1)S(1)} %get-tuple-element.4, bf16[1,4096,2304]{1,2,0:T(8,128)(2,1)} %all-gather.30.cloned.1.call-done), kind=kOutput, calls=%fused_computation.6 | convolution fusion | flops 4831838208 | bytes 23330816 | tf_op jit(solution)/shard_map/dot_general | solution.py:70
  368.0 2.3 broadcast_select_fusion
  370.3 108.7 %all-gather.32.cloned.1.call-done = bf16[1,4096,2304]{1,2,0:T(8,128)(2,1)} async-done(((bf16[1,4096,576]{1,2,0:T(8,128)(2,1)}), bf16[1,4096,2304]{1,2,0:T(8,128)(2,1)}) %all-gather.32.cloned.1.call-update) | async-done | bytes 18874384 | tf_op jit(solution)/shard_map/all_gather | solution.py:67
  479.0 11.3 %fusion.35 = f32[256,2304]{1,0:T(8,128)} fusion(f32[256,2304]{1,0:T(8,128)} %fusion.6, bf16[256,4096]{1,0:T(8,128)(2,1)S(1)} %broadcast_select_fusion, bf16[1,4096,2304]{1,2,0:T(8,128)(2,1)} %all-gather.32.cloned.1.call-done), kind=kOutput, calls=%fused_computation.31 | convolution fusion | flops 4832428032 | bytes 25690112 | tf_op jit(solution)/shard_map/dot_general | solution.py:71
  490.3 61.0 %all-gather.36.cloned.1.call-done = bf16[1,2304,2304]{2,1,0:T(8,128)(2,1)} async-done(((bf16[1,576,2304]{2,1,0:T(8,128)(2,1)}), bf16[1,2304,2304]{2,1,0:T(8,128)(2,1)}) %all-gather.36.cloned.1.call-update) | async-done | bytes 10616848 | tf_op jit(solution)/shard_map/all_gather | solution.py:52
  551.4 72.5 %all-gather.38.cloned.1.call-done = bf16[1,2304,2304]{1,2,0:T(8,128)(2,1)} async-done(((bf16[1,2304,576]{1,2,0:T(8,128)(2,1)}), bf16[1,2304,2304]{1,2,0:T(8,128)(2,1)}) %all-gather.38.cloned.1.call-update) | async-done | bytes 10616848 | tf_op jit(solution)/shard_map/all_gather | solution.py:74
  623.9 16.2 %fusion.32 = f32[256,2304]{1,0:T(8,128)} fusion(f32[256,2304]{1,0:T(8,128)} %fusion.35, bf16[1,2304,2304]{1,2,0:T(8,128)(2,1)} %all-gather.38.cloned.1.call-done, f32[256,2304]{1,0:T(8,128)} %fusion.50, bf16[256,2304]{0,1:T(8,128)(2,1)} %fusion.43, bf16[1,2304,2304]{2,1,0:T(8,128)(2,1)} %all-gather.36.cloned.1.call-done), kind=kOutput, calls=%fused_computation.30 | convolution fusion | flops 5437587456 | bytes 29491200 | tf_op jit(solution)/shard_map/dot_general | solution.py:72
  640.1 0.7 all-gather.24.cloned.1.call-update
  640.9 0.5 all-gather.22.cloned.1.call-update
  641.4 165.5 %all-gather.40.cloned.1.call-done = f32[1024,2304]{1,0:T(8,128)} async-done(((f32[256,2304]{1,0:T(8,128)}), f32[1024,2304]{1,0:T(8,128)}) %all-gather.40.cloned.1.call-update) | async-done | bytes 9437200 | tf_op jit(solution)/shard_map/all_gather | solution.py:78
  807.0 4.4 reduce_sum.28
  811.4 12.8 %fusion.22 = bf16[256,4096]{1,0:T(8,128)(2,1)S(1)} fusion(bf16[256,2304]{1,0:T(8,128)(2,1)S(1)} %reduce_sum.28, bf16[1,4096,2304]{1,2,0:T(8,128)(2,1)} %all-gather.32.cloned.1.call-done), kind=kOutput, calls=%fused_computation.22 | convolution fusion | flops 4832886784 | bytes 22151168 | tf_op jit(solution)/shard_map/dot_general | solution.py:80
  824.3 1.3 collective-permute-start.1
  825.6 48.2 %collective-permute-done.1 = bf16[256,4096]{1,0:T(8,128)(2,1)S(1)} collective-permute-done((bf16[256,4096]{1,0:T(8,128)(2,1)S(1)}, bf16[256,4096]{1,0:T(8,128)(2,1)S(1)}, u32[]{:S(2)}, u32[]{:S(2)}) %collective-permute-start.1) | collective-permute-done | bytes 2097184 | tf_op jit(solution)/shard_map/ppermute | solution.py:14
  873.7 18.3 %fusion.28 = bf16[256,4096]{1,0:T(8,128)(2,1)} fusion(f32[256,4096]{1,0:T(8,128)S(1)} %copy-done.5, bf16[256,4096]{1,0:T(8,128)(2,1)S(1)} %collective-permute-done.1, f32[32,8,32,128]{3,2,1,0:T(8,128)S(1)} %bitcast.95, bf16[256,2304]{1,0:T(8,128)(2,1)S(1)} %reduce_sum.28, bf16[1,4096,2304]{1,2,0:T(8,128)(2,1)} %all-gather.30.cloned.1.call-done), kind=kOutput, calls=%fused_computation.28 | convolution fusion | flops 4839178240 | bytes 32636928 | tf_op jit(solution)/shard_map/dot_general | solution.py:79
  892.1 3.5 all-to-all-start
  895.6 1.4 copy.18
  897.0 27.4 %all-to-all-done = bf16[256,4,576]{0,2,1:T(8,128)(2,1)S(1)} async-done(((bf16[256,4,576]{0,2,1:T(8,128)(2,1)}), bf16[256,4,576]{0,2,1:T(8,128)(2,1)S(1)}, u32[]{:S(2)}, u32[]{:S(2)}) %all-to-all-start) | async-done | bytes 1179680 | tf_op jit(solution)/shard_map/all_to_all | solution.py:85
  924.5 3.8 all-to-all-start.1
  928.3 0.1 copy.20
  928.4 19.8 %all-to-all-done.1 = bf16[256,4,576]{0,2,1:T(8,128)(2,1)S(1)} async-done(((bf16[256,4,576]{0,2,1:T(8,128)(2,1)}), bf16[256,4,576]{0,2,1:T(8,128)(2,1)S(1)}, u32[]{:S(2)}, u32[]{:S(2)}) %all-to-all-start.1) | async-done | bytes 1179680 | tf_op jit(solution)/shard_map/all_to_all | solution.py:86
  948.2 0.1 copy.21
  948.4 10.9 %multiply_bitcast_fusion = f32[1,4096,576]{1,2,0:T(8,128)} fusion(bf16[1024,576]{0,1:T(8,128)(2,1)S(1)} %bitcast.100, bf16[1024,4096]{1,0:T(8,128)(2,1)} %all-gather.24.cloned.1.call-done), kind=kOutput, calls=%fused_computation.17 | convolution fusion | flops 4834197504 | bytes 19005440 | tf_op jit(solution)/shard_map/dot_general | solution.py:95
  959.3 12.1 %multiply_bitcast_fusion.1 = f32[1,4096,576]{1,2,0:T(8,128)} fusion(bf16[1024,576]{0,1:T(8,128)(2,1)S(1)} %bitcast.101, bf16[1024,4096]{1,0:T(8,128)(2,1)} %all-gather.22.cloned.1.call-done), kind=kOutput, calls=%fused_computation.18 | convolution fusion | flops 4834197504 | bytes 19005440 | tf_op jit(solution)/shard_map/dot_general | solution.py:94
  971.4 39.0 %all-gather.20.cloned.1.call-done = bf16[1024,4096]{1,0:T(8,128)(2,1)} async-done(((bf16[256,4096]{1,0:T(8,128)(2,1)}), bf16[1024,4096]{1,0:T(8,128)(2,1)}) %all-gather.20.cloned.1.call-update) | async-done | bytes 8388624 | tf_op jit(solution)/shard_map/all_gather | solution.py:91
  1010.5 5.3 convert_reduce_fusion
  1015.8 0.4 copy-done.4
  1016.2 7.5 convolution_bitcast_fusion
  (40 shorter events, 0.6 us)
Async XLA Ops:
  7.2 35.6 %all-gather.26.cloned.1.call-start = ((), (), s32[]{:S(2)}) async-start(), calls=%async_computation.5 | async-start | bytes 1474560 | tf_op jit(solution)/shard_map/all_gather | solution.py:39
  7.9 155.7 %all-gather.28.cloned.1.call-start = ((), (), s32[]{:S(2)}) async-start(), calls=%async_computation.6 | async-start | bytes 23592960 | tf_op jit(solution)/shard_map/all_gather | solution.py:53
  8.6 227.4 %all-gather.34.cloned.1.call-start = ((), (), s32[]{:S(2)}) async-start(), calls=%async_computation.9 | async-start | bytes 13271040 | tf_op jit(solution)/shard_map/all_gather | solution.py:51
  9.4 348.2 %all-gather.30.cloned.1.call-start = ((), (), s32[]{:S(2)}) async-start(), calls=%async_computation.7 | async-start | bytes 23592960 | tf_op jit(solution)/shard_map/all_gather | solution.py:66
  10.0 469.0 %all-gather.32.cloned.1.call-start = ((), (), s32[]{:S(2)}) async-start(), calls=%async_computation.8 | async-start | bytes 23592960 | tf_op jit(solution)/shard_map/all_gather | solution.py:67
  10.5 1.4 copy-start.9
  10.6 2.7 copy-start.7
  10.6 17.0 %copy-start.8 = (s32[1,2,32]{2,1,0:T(2,128)S(1)}, s32[1,2,32]{2,1,0:T(2,128)}, u32[]{:S(2)}) copy-start(s32[1,2,32]{2,1,0:T(2,128)} %param.14) | copy-start | bytes 772
  10.6 540.8 %all-gather.36.cloned.1.call-start = ((), (), s32[]{:S(2)}) async-start(), calls=%async_computation.10 | async-start | bytes 13271040 | tf_op jit(solution)/shard_map/all_gather | solution.py:52
  11.2 612.7 %all-gather.38.cloned.1.call-start = ((), (), s32[]{:S(2)}) async-start(), calls=%async_computation.11 | async-start | bytes 13271040 | tf_op jit(solution)/shard_map/all_gather | solution.py:74
  11.9 795.1 %all-gather.40.cloned.1.call-start = ((), (), s32[]{:S(2)}) async-start(), calls=%async_computation.12 | async-start | bytes 11796480 | tf_op jit(solution)/shard_map/all_gather | solution.py:78
  47.0 117.1 %copy-start.6 = (f32[1,4096]{1,0:T(1,128)S(1)}, f32[1,4096]{1,0:T(1,128)}, u32[]{:S(2)}) copy-start(f32[1,4096]{1,0:T(1,128)} %param.19) | copy-start | bytes 49156
  164.2 16.1 %copy-start = (f32[2,128,32,128]{3,2,1,0:T(8,128)}, f32[2,128,32,128]{3,2,1,0:T(8,128)S(1)}, u32[]{:S(2)}) copy-start(f32[2,128,32,128]{3,2,1,0:T(8,128)S(1)} %broadcast_in_dim.20) | copy-start | bytes 12582916
  180.3 177.3 %copy-start.2 = (bf16[256,4096]{1,0:T(8,128)(2,1)}, bf16[256,4096]{1,0:T(8,128)(2,1)S(1)}, u32[]{:S(2)}) copy-start(bf16[256,4096]{1,0:T(8,128)(2,1)S(1)} %get-tuple-element.4) | copy-start | bytes 6291460
  180.3 187.7 %collective-permute-start = (bf16[256,4096]{1,0:T(8,128)(2,1)S(1)}, bf16[256,4096]{1,0:T(8,128)(2,1)}, u32[]{:S(2)}, u32[]{:S(2)}) collective-permute-start(bf16[256,4096]{1,0:T(8,128)(2,1)S(1)} %get-tuple-element.4), channel_id=1, source_target_pairs={{0,16},{1,17},{2,18},{3,19},{4,20},{5,21},{6,22},{7,23},{8,24},{9,... | collective-permute-start | bytes 6291464 | tf_op jit(solution)/shard_map/ppermute | solution.py:14
  370.3 120.1 %copy-start.3 = (bf16[256,4096]{1,0:T(8,128)(2,1)}, bf16[256,4096]{1,0:T(8,128)(2,1)S(1)}, u32[]{:S(2)}) copy-start(bf16[256,4096]{1,0:T(8,128)(2,1)S(1)} %broadcast_select_fusion) | copy-start | bytes 6291460
  640.1 308.3 %all-gather.24.cloned.1.call-start = ((), (), s32[]{:S(2)}) async-start(), calls=%async_computation.4 | async-start | bytes 10485760 | tf_op jit(solution)/shard_map/all_gather | solution.py:89
  640.8 318.5 %all-gather.22.cloned.1.call-start = ((), (), s32[]{:S(2)}) async-start(), calls=%async_computation.3 | async-start | bytes 10485760 | tf_op jit(solution)/shard_map/all_gather | solution.py:88
  641.4 369.1 %all-gather.20.cloned.1.call-start = ((), (), s32[]{:S(2)}) async-start(), calls=%async_computation.2 | async-start | bytes 10485760 | tf_op jit(solution)/shard_map/all_gather | solution.py:91
  811.4 62.3 %copy-start.1 = (f32[2,128,32,128]{3,2,1,0:T(8,128)S(1)}, f32[2,128,32,128]{3,2,1,0:T(8,128)}, u32[]{:S(2)}) copy-start(f32[2,128,32,128]{3,2,1,0:T(8,128)} %copy-done) | copy-start | bytes 12582916
  811.4 62.3 %copy-start.5 = (f32[256,4096]{1,0:T(8,128)S(1)}, f32[256,4096]{1,0:T(8,128)}, u32[]{:S(2)}) copy-start(f32[256,4096]{1,0:T(8,128)} %get-tuple-element.5) | copy-start | bytes 12582916
  824.3 49.5 %collective-permute-start.1 = (bf16[256,4096]{1,0:T(8,128)(2,1)S(1)}, bf16[256,4096]{1,0:T(8,128)(2,1)S(1)}, u32[]{:S(2)}, u32[]{:S(2)}) collective-permute-start(bf16[256,4096]{1,0:T(8,128)(2,1)S(1)} %fusion.22), channel_id=1, source_target_pairs={{16,0},{17,1},{18,2},{19,3},{20,4},{21,5},{22,6},{23,7},{24,8},{25... | collective-permute-start | bytes 6291464 | tf_op jit(solution)/shard_map/ppermute | solution.py:14
  892.1 32.4 %all-to-all-start = ((bf16[256,4,576]{0,2,1:T(8,128)(2,1)}), bf16[256,4,576]{0,2,1:T(8,128)(2,1)S(1)}, u32[]{:S(2)}, u32[]{:S(2)}) async-start(bf16[256,4,576]{0,2,1:T(8,128)(2,1)} %bitcast.3), calls=%async_computation | async-start | bytes 2359296 | tf_op jit(solution)/shard_map/all_to_all | solution.py:85
  924.5 23.8 %all-to-all-start.1 = ((bf16[256,4,576]{0,2,1:T(8,128)(2,1)}), bf16[256,4,576]{0,2,1:T(8,128)(2,1)S(1)}, u32[]{:S(2)}, u32[]{:S(2)}) async-start(bf16[256,4,576]{0,2,1:T(8,128)(2,1)} %bitcast.16), calls=%async_computation.1 | async-start | bytes 2359296 | tf_op jit(solution)/shard_map/all_to_all | solution.py:86
  1010.5 5.8 copy-start.4
Sparse Core Ops, SparseCore 0:
  9.5 33.1 all-gather.25
  44.3 119.2 all-gather.27
  165.1 70.9 all-gather.33
  237.5 119.9 all-gather.29
  359.0 119.9 all-gather.31
  480.4 70.9 all-gather.35
  552.9 70.9 all-gather.37
  640.2 166.7 all-gather.39
  808.5 56.4 all-gather.23
  866.4 75.3 all-gather.21
  944.0 66.4 all-gather.19
